TPU v7x, 32 devices: a whole 2x2x4 slice. The times are simulated.
32 devices in a mesh: dp: 16 (over z, y, x), head: 2 (over core).
Axes of the slice: x: 2, y: 2, z: 4, core: 2. Of those that a mesh axis runs over, the one named last changes fastest.
Arguments:
- inputs: bfloat16 [16, 2, 512, 768], P('dp'), may hold values from -6 to 6
- cotangent: bfloat16 [16, 2, 512, 768], P('dp'), may hold values from -6 to 6
- seg_counts: int32 [16], P('dp'), may hold values from 1 to 2
- qkv_weight: float32 [3, 768, 768], P(None, 'dp', 'head'), may hold values from -0.3125 to 0.3125
- out_weight: float32 [768, 768], P('head', 'dp'), may hold values from -0.875 to 0.875
- up_weight: float32 [768, 3072], P('dp', 'head'), may hold values from -0.21875 to 0.21875
- down_weight: float32 [3072, 768], P('head', 'dp'), may hold values from -0.109375 to 0.109375
- head_bias: float32 [2, 2304], P('head'), may hold values from -3 to 3
- shared_params: float32 [16, 768], replicated, may hold values from -5 to 5
- qkv_first: float32 [3, 768, 768], P(None, 'dp', 'head'), may hold values from -0.00024414062 to 0.00024414062
- out_first: float32 [768, 768], P('head', 'dp'), may hold values from -0.00024414062 to 0.00024414062
- up_first: float32 [768, 3072], P('dp', 'head'), may hold values from -0.00024414062 to 0.00024414062
- down_first: float32 [3072, 768], P('head', 'dp'), may hold values from -0.00024414062 to 0.00024414062
- bias_first: float32 [2, 2304], P('head'), may hold values from -0.00024414062 to 0.00024414062
- shared_first: float32 [16, 768], replicated, may hold values from -0.00024414062 to 0.00024414062
- qkv_second: float32 [3, 768, 768], P(None, 'dp', 'head'), may hold values from 1.4094861e-10 to 5.6379446e-10
- out_second: float32 [768, 768], P('head', 'dp'), may hold values from 1.4094861e-10 to 5.6379446e-10
- up_second: float32 [768, 3072], P('dp', 'head'), may hold values from 1.4094861e-10 to 5.6379446e-10
- down_second: float32 [3072, 768], P('head', 'dp'), may hold values from 1.4094861e-10 to 5.6379446e-10
- bias_second: float32 [2, 2304], P('head'), may hold values from 1.4094861e-10 to 5.6379446e-10
- shared_second: float32 [16, 768], replicated, may hold values from 1.4094861e-10 to 5.6379446e-10
Outputs:
- outputs: bfloat16 [16, 2, 512, 768], P('dp')
- input_grad: bfloat16 [16, 2, 512, 768], P('dp')
- grad_norm: float32 [], replicated
- qkv_update: float32 [3, 768, 768], P(None, 'dp', 'head')
- out_update: float32 [768, 768], P('head', 'dp')
- up_update: float32 [768, 3072], P('dp', 'head')
- down_update: float32 [3072, 768], P('head', 'dp')
- bias_update: float32 [2, 2304], P('head')
- shared_update: float32 [16, 768], replicated
- qkv_moment: float32 [3, 768, 768], P(None, 'dp', 'head')
- out_moment: float32 [768, 768], P('head', 'dp')
- up_moment: float32 [768, 3072], P('dp', 'head')
- down_moment: float32 [3072, 768], P('head', 'dp')
- bias_moment: float32 [2, 2304], P('head')
- shared_moment: float32 [16, 768], replicated
- qkv_square: float32 [3, 768, 768], P(None, 'dp', 'head')
- out_square: float32 [768, 768], P('head', 'dp')
- up_square: float32 [768, 3072], P('dp', 'head')
- down_square: float32 [3072, 768], P('head', 'dp')
- bias_square: float32 [2, 2304], P('head')
- shared_square: float32 [16, 768], replicated
Inputs may be any that keep to these rules, and one draw needn't show every extreme that they name: `seg_counts`: a chain's slots 0 to its count minus 1 are live.
All inputs are finite; a program needn't handle non-finite values.
Results may differ from a plain program's by a relative error of at most 0.02.
The roundings to bfloat16 on the way count: a program that leaves them out, or rounds other values in their place, can miss the bound.
Values may be sent and summed in bfloat16 or wider, within the bound.
No kernel may reach another device: no remote copies, remote signals or barrier semaphores. Data moves between devices by JAX's collectives and lax.ppermute only.
A program may use at most 192 MiB of HBM per device.

v0:
```python
import jax
import jax.numpy as jnp
from jax import lax
from jax.sharding import PartitionSpec as P

HD = 64
STEP = 10
EPSILON = 1e-06
BETA_ONE = 0.9
BETA_TWO = 0.999
LEARN_RATE = 0.1
VECTOR_RATE = 0.6
DECAY_RATE = 0.01
ADAM_EPSILON = 1e-08
CLIP_NORM = 1.0


def norm_rows(values, gain, shift):
    average = jnp.mean(values, axis=-1, keepdims=True)
    centered = values - average
    variance = jnp.mean(centered * centered, axis=-1, keepdims=True)
    return centered * lax.rsqrt(variance + EPSILON) * gain + shift


def gelu_exact(values):
    return jax.nn.gelu(values, approximate=False)


def adam_update(weight, first_old, second_old, gradient, factor, decay_rate, step_rate):
    clipped = gradient * factor
    first_new = BETA_ONE * first_old + (1.0 - BETA_ONE) * clipped
    second_new = BETA_TWO * second_old + (1.0 - BETA_TWO) * clipped * clipped
    first_hat = first_new / (1.0 - BETA_ONE**STEP)
    second_hat = second_new / (1.0 - BETA_TWO**STEP)
    weight_new = weight - step_rate * (
        first_hat / (jnp.sqrt(second_hat) + ADAM_EPSILON) + decay_rate * weight
    )
    return (weight_new, first_new, second_new)


def square_sum(arrays):
    return sum((jnp.sum(member * member) for member in arrays))


def shards(
    inputs,
    cotangent,
    seg_counts,
    qkv_weight,
    out_weight,
    up_weight,
    down_weight,
    head_bias,
    shared_params,
    qkv_first,
    out_first,
    up_first,
    down_first,
    bias_first,
    shared_first,
    qkv_second,
    out_second,
    up_second,
    down_second,
    bias_second,
    shared_second,
):
    chains, segments, seg_len, model_width = inputs.shape
    mem_count = shared_params.shape[0] - 6
    seg_rows = seg_len + 2 * mem_count
    local_width = qkv_weight.shape[2]
    head_local = local_width // HD
    score_scale = HD ** (-0.5)
    bfloat = jnp.bfloat16
    single = jnp.float32
    qkv_full, out_full, up_full, down_full = (
        lax.all_gather(qkv_weight.astype(bfloat), "dp", axis=1, tiled=True),
        lax.all_gather(out_weight.astype(bfloat), "dp", axis=1, tiled=True),
        lax.all_gather(up_weight.astype(bfloat), "dp", axis=0, tiled=True),
        lax.all_gather(down_weight.astype(bfloat), "dp", axis=1, tiled=True),
    )
    q_bias = head_bias[0, :local_width]
    v_bias = head_bias[0, local_width : 2 * local_width]
    up_bias = head_bias[0, 2 * local_width :]
    out_bias = shared_params[mem_count]
    down_bias = shared_params[mem_count + 1]
    gain_one = shared_params[mem_count + 2]
    shift_one = shared_params[mem_count + 3]
    gain_two = shared_params[mem_count + 4]
    shift_two = shared_params[mem_count + 5]
    alive_all = (jnp.arange(segments, dtype=jnp.int32)[None, :] < seg_counts[:, None]).astype(
        single
    )
    memory = shared_params[:mem_count][None]
    stored = []
    token_list = []
    for segment in range(segments):
        alive_mask = alive_all[:, segment][:, None, None]
        layer_in = jnp.concatenate([memory, inputs[:, segment].astype(single), memory], axis=1)
        layer_low = layer_in.astype(bfloat)
        projected = jnp.einsum("cld,tde->tcle", layer_low, qkv_full, preferred_element_type=single)
        query_low = (projected[0] + q_bias).astype(bfloat).reshape(chains, seg_rows, head_local, HD)
        key_low = projected[1].astype(bfloat).reshape(chains, seg_rows, head_local, HD)
        value_low = (projected[2] + v_bias).astype(bfloat).reshape(chains, seg_rows, head_local, HD)
        scores = (
            jnp.einsum("cqhe,ckhe->chqk", query_low, key_low, preferred_element_type=single)
            * score_scale
        )
        log_total = jax.nn.logsumexp(scores, axis=-1, keepdims=True)
        chance_low = jnp.exp(scores - log_total).astype(bfloat)
        context_low = (
            jnp.einsum("chqk,ckhe->cqhe", chance_low, value_low, preferred_element_type=single)
            .reshape(chains, seg_rows, local_width)
            .astype(bfloat)
        )
        attn_part = jnp.einsum("cle,ed->cld", context_low, out_full, preferred_element_type=single)
        attn_out = lax.psum(attn_part.astype(jnp.bfloat16), "head").astype(jnp.float32)
        first_in = layer_in + attn_out + out_bias
        hidden = norm_rows(first_in, gain_one, shift_one)
        hidden_low = hidden.astype(bfloat)
        upper_in = (
            jnp.einsum("cld,de->cle", hidden_low, up_full, preferred_element_type=single) + up_bias
        )
        active_low = gelu_exact(upper_in).astype(bfloat)
        ffn_part = jnp.einsum("cle,ed->cld", active_low, down_full, preferred_element_type=single)
        ffn_out = lax.psum(ffn_part.astype(jnp.bfloat16), "head").astype(jnp.float32)
        second_in = hidden + ffn_out + down_bias
        result = norm_rows(second_in, gain_two, shift_two)
        token_list.append(result[:, mem_count : mem_count + seg_len] * alive_mask)
        memory = jnp.where(alive_mask > 0, result[:, mem_count + seg_len :], memory)
        stored.append(
            (
                layer_in,
                query_low,
                key_low,
                value_low,
                log_total,
                context_low,
                first_in,
                hidden,
                upper_in,
                active_low,
                second_in,
            )
        )
    outputs = jnp.stack(token_list, axis=1).astype(bfloat)
    grad_qkv = jnp.zeros(qkv_full.shape, single)
    grad_out = jnp.zeros(out_full.shape, single)
    grad_up = jnp.zeros(up_full.shape, single)
    grad_down = jnp.zeros(down_full.shape, single)
    grad_qbias = jnp.zeros((local_width,), single)
    grad_vbias = jnp.zeros((local_width,), single)
    grad_upbias = jnp.zeros(up_bias.shape, single)
    vector_grads = jnp.zeros((6, model_width), single)
    memory_grad = jnp.zeros((chains, mem_count, model_width), single)
    grad_list = [None] * segments
    for segment in reversed(range(segments)):
        (
            layer_in,
            query_low,
            key_low,
            value_low,
            log_total,
            context_low,
            first_in,
            hidden,
            upper_in,
            active_low,
            second_in,
        ) = stored[segment]
        alive_mask = alive_all[:, segment][:, None, None]
        result_grad = jnp.concatenate(
            [
                jnp.zeros((chains, mem_count, model_width), single),
                cotangent[:, segment].astype(single) * alive_mask,
                memory_grad * alive_mask,
            ],
            axis=1,
        )
        unused, norm_two_back = jax.vjp(norm_rows, second_in, gain_two, shift_two)
        second_grad, gain_two_grad, shift_two_grad = norm_two_back(result_grad)
        ffn_grad_low = second_grad.astype(bfloat)
        grad_down = grad_down + jnp.einsum(
            "cle,cld->ed", active_low, ffn_grad_low, preferred_element_type=single
        )
        active_grad = jnp.einsum(
            "cld,ed->cle", ffn_grad_low, down_full, preferred_element_type=single
        )
        unused, gelu_back = jax.vjp(gelu_exact, upper_in)
        (upper_grad,) = gelu_back(active_grad)
        grad_upbias = grad_upbias + jnp.sum(upper_grad, axis=(0, 1))
        upper_low = upper_grad.astype(bfloat)
        hidden_low = hidden.astype(bfloat)
        grad_up = grad_up + jnp.einsum(
            "cld,cle->de", hidden_low, upper_low, preferred_element_type=single
        )
        hidden_part = jnp.einsum("cle,de->cld", upper_low, up_full, preferred_element_type=single)
        hidden_grad = second_grad + lax.psum(hidden_part.astype(jnp.bfloat16), "head").astype(
            jnp.float32
        )
        unused, norm_one_back = jax.vjp(norm_rows, first_in, gain_one, shift_one)
        first_grad, gain_one_grad, shift_one_grad = norm_one_back(hidden_grad)
        attn_low = first_grad.astype(bfloat)
        grad_out = grad_out + jnp.einsum(
            "cle,cld->ed", context_low, attn_low, preferred_element_type=single
        )
        context_grad = jnp.einsum("cld,ed->cle", attn_low, out_full, preferred_element_type=single)
        context_grad = context_grad.astype(bfloat).reshape(chains, seg_rows, head_local, HD)
        chance_grad = jnp.einsum(
            "cqhe,ckhe->chqk", context_grad, value_low, preferred_element_type=single
        )
        scores = (
            jnp.einsum("cqhe,ckhe->chqk", query_low, key_low, preferred_element_type=single)
            * score_scale
        )
        chances = jnp.exp(scores - log_total)
        value_grad = jnp.einsum(
            "chqk,cqhe->ckhe", chances.astype(bfloat), context_grad, preferred_element_type=single
        )
        weighted = jnp.sum(chances * chance_grad, axis=-1, keepdims=True)
        score_low = (chances * (chance_grad - weighted)).astype(bfloat)
        query_grad = (
            jnp.einsum("chqk,ckhe->cqhe", score_low, key_low, preferred_element_type=single)
            * score_scale
        )
        key_grad = (
            jnp.einsum("chqk,cqhe->ckhe", score_low, query_low, preferred_element_type=single)
            * score_scale
        )
        query_grad = query_grad.reshape(chains, seg_rows, local_width)
        key_grad = key_grad.reshape(chains, seg_rows, local_width)
        value_grad = value_grad.reshape(chains, seg_rows, local_width)
        grad_qbias = grad_qbias + jnp.sum(query_grad, axis=(0, 1))
        grad_vbias = grad_vbias + jnp.sum(value_grad, axis=(0, 1))
        project_low = jnp.stack([query_grad, key_grad, value_grad]).astype(bfloat)
        grad_qkv = grad_qkv + jnp.einsum(
            "cld,tcle->tde", layer_in.astype(bfloat), project_low, preferred_element_type=single
        )
        rows_part = jnp.einsum(
            "tcle,tde->cld", project_low, qkv_full, preferred_element_type=single
        )
        rows_grad = first_grad + lax.psum(rows_part.astype(jnp.bfloat16), "head").astype(
            jnp.float32
        )
        grad_list[segment] = rows_grad[:, mem_count : mem_count + seg_len] * alive_mask
        memory_new = rows_grad[:, :mem_count] + rows_grad[:, mem_count + seg_len :]
        memory_grad = jnp.where(alive_mask > 0, memory_new, memory_grad)
        vector_grads = vector_grads + jnp.stack(
            [
                jnp.sum(first_grad, axis=(0, 1)),
                jnp.sum(second_grad, axis=(0, 1)),
                gain_one_grad,
                shift_one_grad,
                gain_two_grad,
                shift_two_grad,
            ]
        )
    input_grad = jnp.stack(grad_list, axis=1).astype(bfloat)
    head_grad = jnp.concatenate([grad_qbias, grad_vbias, grad_upbias])[None]
    shared_grad = jnp.concatenate([jnp.sum(memory_grad, axis=0), vector_grads], axis=0)
    dp_index = lax.axis_index("dp")
    summed = lax.psum((grad_qkv, grad_out, grad_up, grad_down, head_grad, shared_grad), "dp")
    head_squares = square_sum(summed[:5])
    squares_total = lax.psum(head_squares, "head") + square_sum((summed[5],))
    qkv_block = qkv_weight.shape[1]
    out_block = out_weight.shape[1]
    up_block = up_weight.shape[0]
    down_block = down_weight.shape[1]
    qkv_grad = lax.dynamic_slice_in_dim(summed[0], dp_index * qkv_block, qkv_block, 1)
    out_grad = lax.dynamic_slice_in_dim(summed[1], dp_index * out_block, out_block, 1)
    up_grad = lax.dynamic_slice_in_dim(summed[2], dp_index * up_block, up_block, 0)
    down_grad = lax.dynamic_slice_in_dim(summed[3], dp_index * down_block, down_block, 1)
    bias_grad = summed[4]
    common_grad = summed[5]
    grad_norm = jnp.sqrt(squares_total)
    factor = CLIP_NORM / jnp.maximum(grad_norm, CLIP_NORM)
    qkv_result = adam_update(
        qkv_weight, qkv_first, qkv_second, qkv_grad, factor, DECAY_RATE, LEARN_RATE
    )
    out_result = adam_update(
        out_weight, out_first, out_second, out_grad, factor, DECAY_RATE, LEARN_RATE
    )
    up_result = adam_update(up_weight, up_first, up_second, up_grad, factor, DECAY_RATE, LEARN_RATE)
    down_result = adam_update(
        down_weight, down_first, down_second, down_grad, factor, DECAY_RATE, LEARN_RATE
    )
    bias_result = adam_update(
        head_bias, bias_first, bias_second, bias_grad, factor, 0.0, VECTOR_RATE
    )
    shared_result = adam_update(
        shared_params, shared_first, shared_second, common_grad, factor, 0.0, VECTOR_RATE
    )
    return (
        outputs,
        input_grad,
        grad_norm,
        qkv_result[0],
        out_result[0],
        up_result[0],
        down_result[0],
        bias_result[0],
        shared_result[0],
        qkv_result[1],
        out_result[1],
        up_result[1],
        down_result[1],
        bias_result[1],
        shared_result[1],
        qkv_result[2],
        out_result[2],
        up_result[2],
        down_result[2],
        bias_result[2],
        shared_result[2],
    )


def solution(mesh):
    return jax.shard_map(
        shards,
        mesh=mesh,
        in_specs=(
            P("dp", None, None, None),
            P("dp", None, None, None),
            P("dp"),
            P(None, "dp", "head"),
            P("head", "dp"),
            P("dp", "head"),
            P("head", "dp"),
            P("head", None),
            P(),
            P(None, "dp", "head"),
            P("head", "dp"),
            P("dp", "head"),
            P("head", "dp"),
            P("head", None),
            P(),
            P(None, "dp", "head"),
            P("head", "dp"),
            P("dp", "head"),
            P("head", "dp"),
            P("head", None),
            P(),
        ),
        out_specs=(
            P("dp", None, None, None),
            P("dp", None, None, None),
            P(),
            P(None, "dp", "head"),
            P("head", "dp"),
            P("dp", "head"),
            P("head", "dp"),
            P("head", None),
            P(),
            P(None, "dp", "head"),
            P("head", "dp"),
            P("dp", "head"),
            P("head", "dp"),
            P("head", None),
            P(),
            P(None, "dp", "head"),
            P("head", "dp"),
            P("dp", "head"),
            P("head", "dp"),
            P("head", None),
            P(),
        ),
        check_vma=False,
    )
```

profile of v0, /device:TPU:0, one launch (start us, length us, event | category | flops | bytes accessed | tf_op | source)
XLA Modules:
  0.0 962.0 jit_solution(8777795133562710844)
XLA Ops:
  11.5 47.0 %all_gather.13 = bf16[384,768]{0,1:T(8,128)(2,1)S(1)} all-gather(bf16[384,48]{0,1:T(8,128)(2,1)S(1)} %convert_element_type.373), channel_id=1, replica_groups=mesh['dp'=16,'head'=2] {'dp'}, dimensions={1}, use_global_device_ids=true | all-gather | bytes 626688 | tf_op jit(solution)/shard_map/all_gather | solution.py:78
  61.8 12.4 %all-gather.4.cloned.1.call-done = bf16[3,768,384]{2,1,0:T(8,128)(2,1)} async-done(((bf16[3,48,384]{2,1,0:T(8,128)(2,1)}), bf16[3,768,384]{2,1,0:T(8,128)(2,1)}) %all-gather.4.cloned.1.call-update) | async-done | bytes 1769488 | tf_op jit(solution)/shard_map/all_gather | solution.py:77
  88.4 5.3 convolution_convert_fusion.7
  98.0 16.3 %all-reduce.12.cloned.1.call-done = bf16[1,532,768]{2,1,0:T(8,128)(2,1)} async-done(((bf16[1,532,768]{2,1,0:T(8,128)(2,1)}), bf16[1,532,768]{2,1,0:T(8,128)(2,1)}) %all-reduce.12.cloned.1.call-update) | async-done | bytes 817168 | tf_op jit(solution)/shard_map/psum | solution.py:117
  116.2 65.4 %all-gather.6.cloned.1.call-done = bf16[768,1536]{1,0:T(8,128)(2,1)} async-done(((bf16[48,1536]{1,0:T(8,128)(2,1)}), bf16[768,1536]{1,0:T(8,128)(2,1)}) %all-gather.6.cloned.1.call-update) | async-done | bytes 2359312 | tf_op jit(solution)/shard_map/all_gather | solution.py:79
  181.6 11.6 %multiply_convert_fusion.3 = (bf16[532,1536]{1,0:T(8,128)(2,1)S(1)}, f32[532,1536]{1,0:T(8,128)}, f32[532,1536]{1,0:T(8,128)}) fusion(f32[1536]{0:T(1024)S(1)} %slice_reduce_fusion, bf16[768,1536]{1,0:T(8,128)(2,1)} %all-gather.6.cloned.1.call-done, f32[1,532,768]{2,1,0:T(8,128)S(1)} %get-tuple-element.134, f32[768]{0:T(1024)S(1)} %get-tuple-element.80, ...), kind=kOutput, calls=%fused_computation.37 | convolution fusion | flops 1311120384 | bytes 12181664 | tf_op jit(solution)/shard_map/cld,de->cle/dot_general | solution.py:122
  193.1 53.2 %all-gather.8.cloned.1.call-done = bf16[1536,768]{0,1:T(8,128)(2,1)} async-done(((bf16[1536,48]{0,1:T(8,128)(2,1)}), bf16[1536,768]{0,1:T(8,128)(2,1)}) %all-gather.8.cloned.1.call-update) | async-done | bytes 2359312 | tf_op jit(solution)/shard_map/all_gather | solution.py:80
  246.3 4.0 fusion.32
  252.3 16.3 %all-reduce.14.cloned.1.call-done = bf16[1,532,768]{2,1,0:T(8,128)(2,1)} async-done(((bf16[1,532,768]{2,1,0:T(8,128)(2,1)}), bf16[1,532,768]{2,1,0:T(8,128)(2,1)}) %all-reduce.14.cloned.1.call-update) | async-done | bytes 817168 | tf_op jit(solution)/shard_map/psum | solution.py:126
  282.7 5.3 convolution_convert_fusion.6
  290.7 20.4 %all-reduce.16.cloned.1.call-done = bf16[1,532,768]{2,1,0:T(8,128)(2,1)} async-done(((bf16[1,532,768]{2,1,0:T(8,128)(2,1)}), bf16[1,532,768]{2,1,0:T(8,128)(2,1)}) %all-reduce.16.cloned.1.call-update) | async-done | bytes 817168 | tf_op jit(solution)/shard_map/psum | solution.py:117
  314.0 10.0 %multiply_convert_fusion.2 = (bf16[532,1536]{1,0:T(8,128)(2,1)S(1)}, f32[532,1536]{1,0:T(8,128)}, f32[532,1536]{1,0:T(8,128)}) fusion(f32[1536]{0:T(1024)S(1)} %copy-done.101, bf16[768,1536]{1,0:T(8,128)(2,1)S(1)} %copy-done.102, f32[1,532,768]{2,1,0:T(8,128)S(1)} %get-tuple-element.126, f32[532]{0:T(1024)S(1)} %fusion.77, ...), kind=kOutput, calls=%fused_computation.24 | convolution fusion | flops 1311120384 | bytes 12181664 | tf_op jit(solution)/shard_map/cld,de->cle/dot_general | solution.py:122
  328.4 4.6 fusion.26
  333.0 15.2 %all-reduce.18.cloned.1.call-done = bf16[1,532,768]{2,1,0:T(8,128)(2,1)} async-done(((bf16[1,532,768]{2,1,0:T(8,128)(2,1)}), bf16[1,532,768]{2,1,0:T(8,128)(2,1)}) %all-reduce.18.cloned.1.call-update) | async-done | bytes 817168 | tf_op jit(solution)/shard_map/psum | solution.py:126
  361.4 19.5 %all-reduce.20.cloned.1.call-done = bf16[1,532,768]{2,1,0:T(8,128)(2,1)} async-done(((bf16[1,532,768]{2,1,0:T(8,128)(2,1)}), bf16[1,532,768]{2,1,0:T(8,128)(2,1)}) %all-reduce.20.cloned.1.call-update) | async-done | bytes 817168 | tf_op jit(solution)/shard_map/psum | solution.py:198
  389.4 6.0 fusion.135
  395.4 4.7 multiply_reduce_fusion.1
  412.2 4.1 fusion.38
  416.5 6.3 fusion.99
  422.9 4.3 fusion.50
  429.1 7.8 all-reduce.22.cloned.1.call-done
  440.2 4.5 multiply_reduce_fusion.7
  453.0 4.6 fusion.61
  457.6 6.9 convolution_add_fusion.1
  464.5 8.8 all-reduce.24.cloned.1.call-done
  478.7 5.1 fusion.134
  483.8 4.9 multiply_reduce_fusion
  495.6 3.9 fusion.39
  499.6 7.3 convolution_add_fusion
  514.0 3.7 fusion.54
  523.7 81.7 %all-reduce = (f32[1,2304]{1,0:T(1,128)S(1)}, f32[16,768]{1,0:T(8,128)S(1)}) all-reduce(f32[1,2304]{1,0:T(1,128)S(1)} %broadcast_in_dim.95, f32[16,768]{1,0:T(8,128)S(1)} %pad_maximum_fusion.10), channel_id=1, replica_groups=mesh['dp'=16,'head'=2] {'dp'}, use_global_device_ids=true, to_apply=%region_44.45 | all-reduce | flops 14592 | bytes 116736 | tf_op jit(solution)/shard_map/psum | solution.py:262
  611.9 314.1 %all-reduce.28.cloned.1.call-done = (f32[3,768,384]{2,1,0:T(8,128)}, f32[384,768]{0,1:T(8,128)}, f32[768,1536]{1,0:T(8,128)}, f32[1536,768]{0,1:T(8,128)}) async-done(((f32[3,768,384]{2,1,0:T(8,128)}, f32[384,768]{0,1:T(8,128)}, f32[768,1536]{1,0:T(8,128)}, f32[1536,768]{0,1:T(8,128)}), (f32[3,768,384]{2,1,0:T(8,128)}, f32[384,768]{0,1:T(8,128)}, f32[768,1536]{1,0:T(8,128)}, ...) | async-done | bytes 14155792 | tf_op jit(solution)/shard_map/psum | solution.py:262
  (412 shorter events, 152.0 us)
Async XLA Ops:
  7.2 67.0 %all-gather.4.cloned.1.call-start = ((), (), s32[]{:S(2)}) async-start(), calls=%async_computation | async-start | bytes 1880064 | tf_op jit(solution)/shard_map/all_gather | solution.py:77
  8.9 105.4 %all-reduce.12.cloned.1.call-start = ((), (), s32[]{:S(2)}) async-start(), calls=%async_computation.1 | async-start | bytes 1646592 | tf_op jit(solution)/shard_map/psum | solution.py:117
  9.7 64.5 %copy-start.94 = (bf16[10,768]{1,0:T(8,128)(2,1)}, bf16[10,768]{1,0:T(8,128)(2,1)S(1)}, u32[]{:S(2)}) copy-start(bf16[10,768]{1,0:T(8,128)(2,1)S(1)} %slice.211) | copy-start | bytes 46084
  58.5 35.2 %copy-start.29 = (bf16[384,768]{0,1:T(8,128)(2,1)}, bf16[384,768]{0,1:T(8,128)(2,1)S(1)}, u32[]{:S(2)}) copy-start(bf16[384,768]{0,1:T(8,128)(2,1)S(1)} %all_gather.13) | copy-start | bytes 1769476
  61.8 12.4 %copy-start.53 = (bf16[512,768]{1,0:T(8,128)(2,1)}, bf16[512,768]{1,0:T(8,128)(2,1)S(1)}, u32[]{:S(2)}) copy-start(bf16[512,768]{1,0:T(8,128)(2,1)S(1)} %get-tuple-element.146) | copy-start | bytes 2359300
  96.1 85.5 %all-gather.6.cloned.1.call-start = ((), (), s32[]{:S(2)}) async-start(), calls=%async_computation.2 | async-start | bytes 2506752 | tf_op jit(solution)/shard_map/all_gather | solution.py:79
  96.8 149.5 %all-gather.8.cloned.1.call-start = ((), (), s32[]{:S(2)}) async-start(), calls=%async_computation.3 | async-start | bytes 2506752 | tf_op jit(solution)/shard_map/all_gather | solution.py:80
  97.6 171.0 %all-reduce.14.cloned.1.call-start = ((), (), s32[]{:S(2)}) async-start(), calls=%async_computation.4 | async-start | bytes 1646592 | tf_op jit(solution)/shard_map/psum | solution.py:126
  97.9 83.7 %copy-start.100 = (f32[1536]{0:T(1024)}, f32[1536]{0:T(1024)S(1)}, u32[]{:S(2)}) copy-start(f32[1536]{0:T(1024)S(1)} %slice_reduce_fusion) | copy-start | bytes 18436
  97.9 17.9 %copy-start.86 = (f32[768]{0:T(1024)}, f32[768]{0:T(1024)S(1)}, u32[]{:S(2)}) copy-start(f32[768]{0:T(1024)S(1)} %get-tuple-element.82) | copy-start | bytes 9220
  97.9 170.7 %copy-start.82 = (f32[768]{0:T(1024)}, f32[768]{0:T(1024)S(1)}, u32[]{:S(2)}) copy-start(f32[768]{0:T(1024)S(1)} %get-tuple-element.80) | copy-start | bytes 9220
  98.0 170.7 %copy-start.84 = (f32[768]{0:T(1024)}, f32[768]{0:T(1024)S(1)}, u32[]{:S(2)}) copy-start(f32[768]{0:T(1024)S(1)} %get-tuple-element.79) | copy-start | bytes 9220
  98.0 172.8 %copy-start.80 = (f32[768]{0:T(1024)}, f32[768]{0:T(1024)S(1)}, u32[]{:S(2)}) copy-start(f32[768]{0:T(1024)S(1)} %get-tuple-element.83) | copy-start | bytes 9220
  116.2 76.9 %copy-start.88 = (f32[532]{0:T(1024)}, f32[532]{0:T(1024)S(1)}, u32[]{:S(2)}) copy-start(f32[532]{0:T(1024)S(1)} %multiply_reduce_fusion.18) | copy-start | bytes 6388
  193.1 57.2 %copy-start.34 = (bf16[532,1536]{1,0:T(8,128)(2,1)}, bf16[532,1536]{1,0:T(8,128)(2,1)S(1)}, u32[]{:S(2)}) copy-start(bf16[532,1536]{1,0:T(8,128)(2,1)S(1)} %get-tuple-element.131) | copy-start | bytes 4902916
  250.4 60.6 %all-reduce.16.cloned.1.call-start = ((), (), s32[]{:S(2)}) async-start(), calls=%async_computation.5 | async-start | bytes 1646592 | tf_op jit(solution)/shard_map/psum | solution.py:117
  288.1 22.9 %copy-start.87 = (f32[768]{0:T(1024)S(1)}, f32[768]{0:T(1024)}, u32[]{:S(2)}) copy-start(f32[768]{0:T(1024)} %copy-done.86) | copy-start | bytes 9220
  290.4 57.9 %all-reduce.18.cloned.1.call-start = ((), (), s32[]{:S(2)}) async-start(), calls=%async_computation.6 | async-start | bytes 1646592 | tf_op jit(solution)/shard_map/psum | solution.py:126
  314.0 11.2 %copy-start.105 = (bf16[1536,768]{0,1:T(8,128)(2,1)S(1)}, bf16[1536,768]{0,1:T(8,128)(2,1)}, u32[]{:S(2)}) copy-start(bf16[1536,768]{0,1:T(8,128)(2,1)} %all-gather.8.cloned.1.call-done) | copy-start | bytes 7077892
  327.6 53.3 %all-reduce.20.cloned.1.call-start = ((), (), s32[]{:S(2)}) async-start(), calls=%async_computation.7 | async-start | bytes 1646592 | tf_op jit(solution)/shard_map/psum | solution.py:198
  328.4 19.9 %copy-start.85 = (f32[768]{0:T(1024)S(1)}, f32[768]{0:T(1024)}, u32[]{:S(2)}) copy-start(f32[768]{0:T(1024)} %copy-done.84) | copy-start | bytes 9220
  360.3 76.7 %all-reduce.22.cloned.1.call-start = ((), (), s32[]{:S(2)}) async-start(), calls=%async_computation.8 | async-start | bytes 1646592 | tf_op jit(solution)/shard_map/psum | solution.py:242
  389.4 10.8 %slice-start.2 = ((s8[8232960]{0:T(1024)(128)(4,1)}), s8[4194304]{0:T(1024)(128)(4,1)S(1)}, s32[]{:S(2)}) async-start(s8[8232960]{0:T(1024)(128)(4,1)} %bitcast.210), calls=%async_computation.14 | async-start | bytes 8388608
  416.3 57.0 %all-reduce.24.cloned.1.call-start = ((), (), s32[]{:S(2)}) async-start(), calls=%async_computation.9 | async-start | bytes 1646592 | tf_op jit(solution)/shard_map/psum | solution.py:198
  429.1 11.1 %copy-start.3 = (f32[1,532,768]{2,1,0:T(8,128)S(1)}, f32[1,532,768]{2,1,0:T(8,128)}, u32[]{:S(2)}) copy-start(f32[1,532,768]{2,1,0:T(8,128)} %copy-done.2) | copy-start | bytes 4902916
  452.7 67.5 %all-reduce.26.cloned.1.call-start = ((), (), s32[]{:S(2)}) async-start(), calls=%async_computation.10 | async-start | bytes 1646592 | tf_op jit(solution)/shard_map/psum | solution.py:242
  457.6 15.7 %copy-start.5 = (f32[1,532,768]{2,1,0:T(8,128)S(1)}, f32[1,532,768]{2,1,0:T(8,128)}, u32[]{:S(2)}) copy-start(f32[1,532,768]{2,1,0:T(8,128)} %copy-done.4) | copy-start | bytes 4902916
  464.5 11.0 %copy-start.89 = (f32[532]{0:T(1024)S(1)}, f32[532]{0:T(1024)}, u32[]{:S(2)}) copy-start(f32[532]{0:T(1024)} %copy-done.88) | copy-start | bytes 6388
  499.6 426.5 %all-reduce.28.cloned.1.call-start = ((), (), s32[]{:S(2)}) async-start(), calls=%async_computation.11 | async-start | bytes 28311552 | tf_op jit(solution)/shard_map/psum | solution.py:262
  936.0 11.9 %copy-start.49 = (f32[48,1536]{1,0:T(8,128)S(1)}, f32[48,1536]{1,0:T(8,128)}, u32[]{:S(2)}) copy-start(f32[48,1536]{1,0:T(8,128)} %param.26) | copy-start | bytes 884740
  936.0 11.9 %copy-start.69 = (f32[48,1536]{1,0:T(8,128)S(1)}, f32[48,1536]{1,0:T(8,128)}, u32[]{:S(2)}) copy-start(f32[48,1536]{1,0:T(8,128)} %param.32) | copy-start | bytes 884740
  936.0 11.9 %copy-start.70 = (f32[48,1536]{1,0:T(8,128)S(1)}, f32[48,1536]{1,0:T(8,128)}, u32[]{:S(2)}) copy-start(f32[48,1536]{1,0:T(8,128)} %param.38) | copy-start | bytes 884740
  (103 other events, 379.6 us)
Sparse Core Ops, SparseCore 0:
  11.3 62.8 all-gather.3
  96.2 18.0 all-reduce.11
  118.0 63.5 all-gather.5
  185.2 61.0 all-gather.7
  250.5 18.0 all-reduce.13
  290.5 20.4 all-reduce.15
  327.7 20.4 all-reduce.17
  360.4 20.4 all-reduce.19
  416.4 20.4 all-reduce.21
  452.8 20.4 all-reduce.23
  499.7 20.4 all-reduce.25
  526.5 399.5 all-reduce.27
where the time goes:
time: 970 us; the launch traced here: 962 us
  waiting for transfers between devices  552 us (57%)
  matrix products  134 us (14%)
  blocking collectives  132 us (14%)
  other arithmetic  76.9 us (8%)
  local copies, waits for them, and re-layouts  41.1 us (4%)
  between operations  24.7 us (3%)
    psum x1, waiting for transfers between devices, shards(): lax.psum((grad_qkv, grad_out, grad_up, grad_down, head_grad, shared_grad)...  314 us
    psum x1, blocking collectives, shards(): lax.psum((grad_qkv, grad_out, grad_up, grad_down, head_grad, shared_grad)...  81.7 us
    all_gather x1, waiting for transfers between devices, shards(): lax.all_gather(up_weight.astype(bfloat), 'dp', axis=0, tiled=True)  65.4 us
    all_gather x1, waiting for transfers between devices, shards(): lax.all_gather(down_weight.astype(bfloat), 'dp', axis=1, tiled=True)  53.2 us
    all_gather x1, blocking collectives, shards(): lax.all_gather(out_weight.astype(bfloat), 'dp', axis=1, tiled=True)  47 us
    psum x2, waiting for transfers between devices, shards(): lax.psum(attn_part.astype(jnp.bfloat16), 'head').astype(jnp.float32)  36.6 us
    psum x2, waiting for transfers between devices, shards(): lax.psum(ffn_part.astype(jnp.bfloat16), 'head').astype(jnp.float32)  31.5 us
    psum x2, waiting for transfers between devices, shards(): lax.psum(hidden_part.astype(jnp.bfloat16), 'head').astype(jnp.float32)  28.3 us
  transfers between devices with their start and end apart: 12, of which 12 were waited for; matrix products, arithmetic and copies ran while one was open for 8% of the time, Pallas kernels for 0%

commit v1 on v0

--- a/solution.py
+++ b/solution.py
@@ -2,6 +2,7 @@
 import jax.numpy as jnp
 from jax import lax
 from jax.sharding import PartitionSpec as P
+from jax.lax import all_gather
 
 HD = 64
 STEP = 10
@@ -13,6 +14,7 @@
 DECAY_RATE = 0.01
 ADAM_EPSILON = 1e-08
 CLIP_NORM = 1.0
+carry_sheet_in = lambda inp: all_gather(inp, "head").sum(axis=0)
 
 
 def norm_rows(values, gain, shift):
@@ -114,7 +116,7 @@
             .astype(bfloat)
         )
         attn_part = jnp.einsum("cle,ed->cld", context_low, out_full, preferred_element_type=single)
-        attn_out = lax.psum(attn_part.astype(jnp.bfloat16), "head").astype(jnp.float32)
+        attn_out = carry_sheet_in(attn_part.astype(jnp.bfloat16)).astype(jnp.float32)
         first_in = layer_in + attn_out + out_bias
         hidden = norm_rows(first_in, gain_one, shift_one)
         hidden_low = hidden.astype(bfloat)

time: 970 us -> 956 us (0.986)
  waiting for transfers between devices: 552 us -> 526 us
    psum x2 -> x0, waiting for transfers between devices: 36.6 us -> none  [shards(): lax.psum(attn_part.astype(jnp.bfloat16), 'head').astype(jnp.float32)]
    all_gather x0 -> x2, waiting for transfers between devices: none -> 17.6 us  [carry_sheet_in = lambda inp: all_gather(inp, 'head').sum(axis=0)]
    unnamed x246 -> x278, local copies, waits for them, and re-layouts: 19.2 us -> 21.9 us
  transfers between devices with their start and end apart: 12 -> 12, of which waited for: 12 -> 12; matrix products, arithmetic and copies ran while one was open for 8% -> 9% of each run, Pallas kernels for 0% -> 0%
where the time goes in v1:
time: 956 us; the launch traced here: 948 us
  waiting for transfers between devices  526 us (55%)
  matrix products  138 us (14%)
  blocking collectives  131 us (14%)
  other arithmetic  81.6 us (9%)
  local copies, waits for them, and re-layouts  44.4 us (5%)
  between operations  24.9 us (3%)
    psum x1, waiting for transfers between devices, shards(): lax.psum((grad_qkv, grad_out, grad_up, grad_down, head_grad, shared_grad)...  314 us
    psum x1, blocking collectives, shards(): lax.psum((grad_qkv, grad_out, grad_up, grad_down, head_grad, shared_grad)...  81.6 us
    all_gather x1, waiting for transfers between devices, shards(): lax.all_gather(up_weight.astype(bfloat), 'dp', axis=0, tiled=True)  61.2 us
    all_gather x1, waiting for transfers between devices, shards(): lax.all_gather(down_weight.astype(bfloat), 'dp', axis=1, tiled=True)  51.8 us
    all_gather x1, blocking collectives, shards(): lax.all_gather(out_weight.astype(bfloat), 'dp', axis=1, tiled=True)  46.8 us
    psum x2, waiting for transfers between devices, shards(): lax.psum(ffn_part.astype(jnp.bfloat16), 'head').astype(jnp.float32)  32.1 us
    psum x2, waiting for transfers between devices, shards(): lax.psum(hidden_part.astype(jnp.bfloat16), 'head').astype(jnp.float32)  27.7 us
    dot_general x2, matrix products, shards(): jnp.einsum('cld,de->cle', hidden_low, up_full, preferred_element_type=sin...  23.1 us
  transfers between devices with their start and end apart: 12, of which 12 were waited for; matrix products, arithmetic and copies ran while one was open for 9% of the time, Pallas kernels for 0%

profile of v1, /device:TPU:0, one launch (start us, length us, event | category | flops | bytes accessed | tf_op | source)
XLA Modules:
  0.0 948.5 jit_solution(16356854883026335976)
XLA Ops:
  12.1 46.8 %all_gather.25 = bf16[384,768]{0,1:T(8,128)(2,1)S(1)} all-gather(bf16[384,48]{0,1:T(8,128)(2,1)S(1)} %convert_element_type.455), channel_id=1, replica_groups=mesh['dp'=16,'head'=2] {'dp'}, dimensions={1}, use_global_device_ids=true | all-gather | bytes 626688 | tf_op jit(solution)/shard_map/all_gather | solution.py:80
  58.9 4.0 convert_bitcast_fusion.3
  62.9 12.1 %all-gather.10.cloned.1.call-done = bf16[3,768,384]{2,1,0:T(8,128)(2,1)} async-done(((bf16[3,48,384]{2,1,0:T(8,128)(2,1)}), bf16[3,768,384]{2,1,0:T(8,128)(2,1)}) %all-gather.10.cloned.1.call-update) | async-done | bytes 1769488 | tf_op jit(solution)/shard_map/all_gather | solution.py:79
  89.2 5.3 convolution_convert_fusion.7
  99.2 6.6 all-gather.16.cloned.1.call-done
  111.4 61.2 %all-gather.12.cloned.1.call-done = bf16[768,1536]{1,0:T(8,128)(2,1)} async-done(((bf16[48,1536]{1,0:T(8,128)(2,1)}), bf16[768,1536]{1,0:T(8,128)(2,1)}) %all-gather.12.cloned.1.call-update) | async-done | bytes 2359312 | tf_op jit(solution)/shard_map/all_gather | solution.py:81
  172.7 12.6 %multiply_convert_fusion.3 = (bf16[532,1536]{1,0:T(8,128)(2,1)}, f32[532,1536]{1,0:T(8,128)}, f32[532,1536]{1,0:T(8,128)}) fusion(f32[1536]{0:T(1024)S(1)} %slice_reduce_fusion, bf16[768,1536]{1,0:T(8,128)(2,1)} %all-gather.12.cloned.1.call-done, f32[768]{0:T(1024)S(1)} %get-tuple-element.101, f32[768]{0:T(1024)S(1)} %get-tuple-element.102, ...), kind=kOutput, calls=%fused_computation.37 | convolution fusion | flops 1313163264 | bytes 12971168 | tf_op jit(solution)/shard_map/cld,de->cle/dot_general | solution.py:124
  185.2 51.8 %all-gather.14.cloned.1.call-done = bf16[1536,768]{0,1:T(8,128)(2,1)} async-done(((bf16[1536,48]{0,1:T(8,128)(2,1)}), bf16[1536,768]{0,1:T(8,128)(2,1)}) %all-gather.14.cloned.1.call-update) | async-done | bytes 2359312 | tf_op jit(solution)/shard_map/all_gather | solution.py:82
  237.0 4.6 fusion.36
  243.7 16.1 %all-reduce.10.cloned.1.call-done = bf16[1,532,768]{2,1,0:T(8,128)(2,1)} async-done(((bf16[1,532,768]{2,1,0:T(8,128)(2,1)}), bf16[1,532,768]{2,1,0:T(8,128)(2,1)}) %all-reduce.10.cloned.1.call-update) | async-done | bytes 817168 | tf_op jit(solution)/shard_map/psum | solution.py:128
  274.6 5.0 convolution_convert_fusion.6
  282.3 11.0 %all-gather.18.cloned.1.call-done = bf16[2,532,768]{2,1,0:T(8,128)(2,1)} async-done(((bf16[1,532,768]{2,1,0:T(8,128)(2,1)}), bf16[2,532,768]{2,1,0:T(8,128)(2,1)}) %all-gather.18.cloned.1.call-update) | async-done | bytes 1634320 | tf_op jit(solution)/shard_map/all_gather | solution.py:17
  300.5 10.5 %multiply_convert_fusion.2 = (bf16[532,1536]{1,0:T(8,128)(2,1)S(1)}, f32[532,1536]{1,0:T(8,128)}, f32[532,1536]{1,0:T(8,128)}) fusion(f32[1536]{0:T(1024)S(1)} %copy-done.118, bf16[768,1536]{1,0:T(8,128)(2,1)S(1)} %copy-done.119, f32[532]{0:T(1024)S(1)} %fusion.89, f32[532]{0:T(1024)S(1)} %broadcast_multiply_fusion.2, f32[768]{0:T(1024)S(1)} %copy-done.105, ...), kind=kOutput, calls=%fused_computation.24 | convolution fusion | flops 1313163264 | bytes 12971168 | tf_op jit(solution)/shard_map/cld,de->cle/dot_general | solution.py:124
  315.5 3.9 fusion.32
  319.4 15.9 %all-reduce.12.cloned.1.call-done = bf16[1,532,768]{2,1,0:T(8,128)(2,1)} async-done(((bf16[1,532,768]{2,1,0:T(8,128)(2,1)}), bf16[1,532,768]{2,1,0:T(8,128)(2,1)}) %all-reduce.12.cloned.1.call-update) | async-done | bytes 817168 | tf_op jit(solution)/shard_map/psum | solution.py:128
  348.5 19.5 %all-reduce.14.cloned.1.call-done = bf16[1,532,768]{2,1,0:T(8,128)(2,1)} async-done(((bf16[1,532,768]{2,1,0:T(8,128)(2,1)}), bf16[1,532,768]{2,1,0:T(8,128)(2,1)}) %all-reduce.14.cloned.1.call-update) | async-done | bytes 817168 | tf_op jit(solution)/shard_map/psum | solution.py:200
  368.0 3.8 multiply_reduce_fusion.10
  377.2 6.0 fusion.143
  383.3 4.7 multiply_reduce_fusion.1
  400.0 4.1 fusion.42
  404.4 6.4 fusion.113
  410.8 4.6 fusion.56
  417.4 7.3 all-reduce.16.cloned.1.call-done
  439.7 4.9 fusion.69
  444.6 7.3 convolution_add_fusion.1
  451.8 8.2 all-reduce.18.cloned.1.call-done
  465.2 5.1 fusion.142
  470.3 5.0 multiply_reduce_fusion
  482.1 3.9 fusion.43
  486.1 7.3 convolution_add_fusion
  510.3 81.6 %all-reduce = (f32[1,2304]{1,0:T(1,128)S(1)}, f32[16,768]{1,0:T(8,128)S(1)}) all-reduce(f32[1,2304]{1,0:T(1,128)S(1)} %broadcast_in_dim.92, f32[16,768]{1,0:T(8,128)S(1)} %pad_maximum_fusion.12), channel_id=1, replica_groups=mesh['dp'=16,'head'=2] {'dp'}, use_global_device_ids=true, to_apply=%region_44.45 | all-reduce | flops 14592 | bytes 116736 | tf_op jit(solution)/shard_map/psum | solution.py:264
  598.4 314.2 %all-reduce.22.cloned.1.call-done = (f32[3,768,384]{2,1,0:T(8,128)}, f32[384,768]{0,1:T(8,128)}, f32[768,1536]{1,0:T(8,128)}, f32[1536,768]{0,1:T(8,128)}) async-done(((f32[3,768,384]{2,1,0:T(8,128)}, f32[384,768]{0,1:T(8,128)}, f32[768,1536]{1,0:T(8,128)}, f32[1536,768]{0,1:T(8,128)}), (f32[3,768,384]{2,1,0:T(8,128)}, f32[384,768]{0,1:T(8,128)}, f32[768,1536]{1,0:T(8,128)}, ...) | async-done | bytes 14155792 | tf_op jit(solution)/shard_map/psum | solution.py:264
  (445 shorter events, 162.4 us)
Async XLA Ops:
  7.2 67.8 %all-gather.10.cloned.1.call-start = ((), (), s32[]{:S(2)}) async-start(), calls=%async_computation | async-start | bytes 1880064 | tf_op jit(solution)/shard_map/all_gather | solution.py:79
  8.9 96.9 %all-gather.16.cloned.1.call-start = ((), (), s32[]{:S(2)}) async-start(), calls=%async_computation.9 | async-start | bytes 2469888 | tf_op jit(solution)/shard_map/all_gather | solution.py:17
  9.8 79.4 %copy-start.86 = (f32[6,64]{1,0:T(8,128)}, f32[6,64]{1,0:T(8,128)S(1)}, u32[]{:S(2)}) copy-start(f32[6,64]{1,0:T(8,128)S(1)} %add.565) | copy-start | bytes 4612
  58.9 35.6 %copy-start.40 = (bf16[384,768]{0,1:T(8,128)(2,1)}, bf16[384,768]{0,1:T(8,128)(2,1)S(1)}, u32[]{:S(2)}) copy-start(bf16[384,768]{0,1:T(8,128)(2,1)S(1)} %all_gather.25) | copy-start | bytes 1769476
  62.9 109.8 %copy-start.14 = (f32[512,768]{1,0:T(8,128)}, f32[512,768]{1,0:T(8,128)S(1)}, u32[]{:S(2)}) copy-start(f32[512,768]{1,0:T(8,128)S(1)} %get-tuple-element.165) | copy-start | bytes 4718596
  96.9 75.7 %all-gather.12.cloned.1.call-start = ((), (), s32[]{:S(2)}) async-start(), calls=%async_computation.1 | async-start | bytes 2506752 | tf_op jit(solution)/shard_map/all_gather | solution.py:81
  97.7 139.3 %all-gather.14.cloned.1.call-start = ((), (), s32[]{:S(2)}) async-start(), calls=%async_computation.2 | async-start | bytes 2506752 | tf_op jit(solution)/shard_map/all_gather | solution.py:82
  98.5 161.4 %all-reduce.10.cloned.1.call-start = ((), (), s32[]{:S(2)}) async-start(), calls=%async_computation.3 | async-start | bytes 1646592 | tf_op jit(solution)/shard_map/psum | solution.py:128
  99.1 73.6 %copy-start.117 = (f32[1536]{0:T(1024)}, f32[1536]{0:T(1024)S(1)}, u32[]{:S(2)}) copy-start(f32[1536]{0:T(1024)S(1)} %slice_reduce_fusion) | copy-start | bytes 18436
  99.2 73.5 %copy-start.84 = (f32[768]{0:T(1024)}, f32[768]{0:T(1024)S(1)}, u32[]{:S(2)}) copy-start(f32[768]{0:T(1024)S(1)} %get-tuple-element.103) | copy-start | bytes 9220
  99.2 160.7 %copy-start.104 = (f32[768]{0:T(1024)}, f32[768]{0:T(1024)S(1)}, u32[]{:S(2)}) copy-start(f32[768]{0:T(1024)S(1)} %get-tuple-element.101) | copy-start | bytes 9220
  99.2 160.7 %copy-start.106 = (f32[768]{0:T(1024)}, f32[768]{0:T(1024)S(1)}, u32[]{:S(2)}) copy-start(f32[768]{0:T(1024)S(1)} %get-tuple-element.100) | copy-start | bytes 9220
  99.2 162.8 %copy-start.96 = (f32[768]{0:T(1024)}, f32[768]{0:T(1024)S(1)}, u32[]{:S(2)}) copy-start(f32[768]{0:T(1024)S(1)} %get-tuple-element.104) | copy-start | bytes 9220
  108.4 64.3 %copy-start.109 = (f32[532]{0:T(1024)}, f32[532]{0:T(1024)S(1)}, u32[]{:S(2)}) copy-start(f32[532]{0:T(1024)S(1)} %broadcast_multiply_fusion.4) | copy-start | bytes 6388
  111.4 73.9 %copy-start.102 = (f32[532]{0:T(1024)}, f32[532]{0:T(1024)S(1)}, u32[]{:S(2)}) copy-start(f32[532]{0:T(1024)S(1)} %get-tuple-element.152) | copy-start | bytes 6388
  111.4 148.5 %copy-start.2 = (f32[1,532,768]{2,1,0:T(8,128)}, f32[1,532,768]{2,1,0:T(8,128)S(1)}, u32[]{:S(2)}) copy-start(f32[1,532,768]{2,1,0:T(8,128)S(1)} %get-tuple-element.153) | copy-start | bytes 4902916
  111.4 148.5 %copy-start.92 = (f32[532]{0:T(1024)}, f32[532]{0:T(1024)S(1)}, u32[]{:S(2)}) copy-start(f32[532]{0:T(1024)S(1)} %fusion.87) | copy-start | bytes 6388
  241.6 51.7 %all-gather.18.cloned.1.call-start = ((), (), s32[]{:S(2)}) async-start(), calls=%async_computation.10 | async-start | bytes 2469888 | tf_op jit(solution)/shard_map/all_gather | solution.py:17
  282.0 13.5 %copy-start.75 = (f32[1,10,768]{2,1,0:T(8,128)S(1)}, f32[1,10,768]{2,1,0:T(8,128)}, u32[]{:S(2)}) copy-start(f32[1,10,768]{2,1,0:T(8,128)} %copy-done.74) | copy-start | bytes 92164
  282.0 13.5 %copy-start.85 = (f32[768]{0:T(1024)S(1)}, f32[768]{0:T(1024)}, u32[]{:S(2)}) copy-start(f32[768]{0:T(1024)} %copy-done.84) | copy-start | bytes 9220
  282.1 53.3 %all-reduce.12.cloned.1.call-start = ((), (), s32[]{:S(2)}) async-start(), calls=%async_computation.4 | async-start | bytes 1646592 | tf_op jit(solution)/shard_map/psum | solution.py:128
  300.5 11.8 %copy-start.122 = (bf16[1536,768]{0,1:T(8,128)(2,1)S(1)}, bf16[1536,768]{0,1:T(8,128)(2,1)}, u32[]{:S(2)}) copy-start(bf16[1536,768]{0,1:T(8,128)(2,1)} %all-gather.14.cloned.1.call-done) | copy-start | bytes 7077892
  314.7 53.3 %all-reduce.14.cloned.1.call-start = ((), (), s32[]{:S(2)}) async-start(), calls=%async_computation.5 | async-start | bytes 1646592 | tf_op jit(solution)/shard_map/psum | solution.py:200
  315.5 19.8 %copy-start.107 = (f32[768]{0:T(1024)S(1)}, f32[768]{0:T(1024)}, u32[]{:S(2)}) copy-start(f32[768]{0:T(1024)} %copy-done.106) | copy-start | bytes 9220
  347.4 77.4 %all-reduce.16.cloned.1.call-start = ((), (), s32[]{:S(2)}) async-start(), calls=%async_computation.6 | async-start | bytes 1646592 | tf_op jit(solution)/shard_map/psum | solution.py:244
  404.1 55.9 %all-reduce.18.cloned.1.call-start = ((), (), s32[]{:S(2)}) async-start(), calls=%async_computation.7 | async-start | bytes 1646592 | tf_op jit(solution)/shard_map/psum | solution.py:200
  439.4 67.3 %all-reduce.20.cloned.1.call-start = ((), (), s32[]{:S(2)}) async-start(), calls=%async_computation.8 | async-start | bytes 1646592 | tf_op jit(solution)/shard_map/psum | solution.py:244
  444.6 15.4 %copy-start.3 = (f32[1,532,768]{2,1,0:T(8,128)S(1)}, f32[1,532,768]{2,1,0:T(8,128)}, u32[]{:S(2)}) copy-start(f32[1,532,768]{2,1,0:T(8,128)} %copy-done.2) | copy-start | bytes 4902916
  486.0 426.5 %all-reduce.22.cloned.1.call-start = ((), (), s32[]{:S(2)}) async-start(), calls=%async_computation.11 | async-start | bytes 28311552 | tf_op jit(solution)/shard_map/psum | solution.py:264
  922.5 11.9 %copy-start.66 = (f32[48,1536]{1,0:T(8,128)S(1)}, f32[48,1536]{1,0:T(8,128)}, u32[]{:S(2)}) copy-start(f32[48,1536]{1,0:T(8,128)} %param.26) | copy-start | bytes 884740
  922.5 11.9 %copy-start.76 = (f32[48,1536]{1,0:T(8,128)S(1)}, f32[48,1536]{1,0:T(8,128)}, u32[]{:S(2)}) copy-start(f32[48,1536]{1,0:T(8,128)} %param.32) | copy-start | bytes 884740
  922.5 11.9 %copy-start.77 = (f32[48,1536]{1,0:T(8,128)S(1)}, f32[48,1536]{1,0:T(8,128)}, u32[]{:S(2)}) copy-start(f32[48,1536]{1,0:T(8,128)} %param.38) | copy-start | bytes 884740
  (119 other events, 451.0 us)
Sparse Core Ops, SparseCore 0:
  11.3 63.6 all-gather.9
  97.1 8.6 all-gather.15
  109.1 63.4 all-gather.11
  175.9 61.0 all-gather.13
  241.7 18.0 all-reduce.9
  282.2 11.1 all-gather.17
  314.8 20.4 all-reduce.11
  347.5 20.4 all-reduce.13
  404.2 20.4 all-reduce.15
  439.5 20.4 all-reduce.17
  486.1 20.4 all-reduce.19
  513.0 399.5 all-reduce.21
